TPU v7x, 128 devices: a whole 4x4x4 slice. The times are simulated.
128 devices in a mesh: rows: 2 (over core), head: 4 (over x), cluster: 16 (over y, z).
Axes of the slice: x: 4, y: 4, z: 4, core: 2. Of those that a mesh axis runs over, the one named last changes fastest.
Arguments:
- queries: bfloat16 [4, 512, 8192], P(None, ('rows', 'cluster'), 'head')
- new_keys: bfloat16 [4, 512, 1024], P(None, ('rows', 'cluster'), 'head'), may hold values from -6 to 6
- new_values: bfloat16 [4, 512, 1024], P(None, ('rows', 'cluster'), 'head'), may hold values from -6 to 6
- key_cache: bfloat16 [512, 8, 256, 128], P(('rows', 'cluster'), 'head'), may hold values from -6 to 6
- value_cache: bfloat16 [512, 8, 256, 128], P(('rows', 'cluster'), 'head'), may hold values from -6 to 6
- lengths: int32 [512], P(('rows', 'cluster')), may hold values from 1 to 256, as said below
- residual_in: bfloat16 [4, 512, 8192], P(None, 'rows', 'cluster')
- out_weight: bfloat16 [8192, 8192], P('head', 'cluster'), may hold values from -0.0625 to 0.0625
- norm_gain: float32 [8192], P('cluster'), may hold values from 0.5 to 1.5
- top_weight: bfloat16 [8192, 80], P('cluster')
- leaf_weight: bfloat16 [80, 8192, 1024], P('cluster', None, ('rows', 'head'))
- cluster_ids: int32 [4, 512, 1], replicated, may hold values from 0 to 79; in each aligned block of 256 rows (0 to 255, 256 to 511, ..., all dimensions but the last counted through in order) at most 12 rows name the same one
- targets: int32 [4, 512], replicated, may hold values from 0 to 1023
Outputs:
- log_prob: float32 [4, 512], P(None, ('rows', 'cluster'))
Inputs may be any that keep to these rules, and one draw needn't show every extreme that they name: `cluster_ids`: in each step and each aligned block of 256 rows, no cluster is named by more than 12 rows, a bound that some block reaches. `lengths`: every device's 16 rows include one of length 256.
All inputs are finite; a program needn't handle non-finite values.
Results may differ from a plain program's by a relative error of at most 0.0011.
Values may be sent and summed in bfloat16 or wider, within the bound.
No kernel may reach another device: no remote copies, remote signals or barrier semaphores. Data moves between devices by JAX's collectives and lax.ppermute only.
A program may use at most 128 MiB of HBM per device.

v0:
```python
import jax
import jax.numpy as jnp
from jax import lax
from jax.sharding import PartitionSpec as P

D = 8192
CLUSTERS = 80
STEPS = 4


def merged(part, axis, combine):
    gathered = jax.tree.map(lambda a: lax.all_gather(a, axis), part)

    def take(source):
        return jax.tree.map(lambda a: lax.dynamic_index_in_dim(a, source, 0, False), gathered)

    return lax.fori_loop(
        1, lax.axis_size(axis), lambda source, state: combine(state, take(source)), take(0)
    )


def combine_totals(first, second):
    peak_a, mass_a, picked_a = first
    peak_b, mass_b, picked_b = second
    peak = jnp.maximum(peak_a, peak_b)
    mass = mass_a * jnp.exp(peak_a - peak) + mass_b * jnp.exp(peak_b - peak)
    return (peak, mass, picked_a + picked_b)


def shards(
    queries,
    new_keys,
    new_values,
    key_cache,
    value_cache,
    lengths,
    residual_in,
    out_weight,
    norm_gain,
    top_weight,
    leaf_weight,
    cluster_ids,
    targets,
):
    own_rows, kv_local, cache_len, head_dim = key_cache.shape
    group = queries.shape[2] // head_dim // kv_local
    scale = head_dim ** (-0.5)
    clusters_axis = lax.axis_size("cluster")
    row_groups = lax.axis_size("rows")
    heads_axis = lax.axis_size("head")
    row_group = own_rows * clusters_axis
    local_clusters = leaf_weight.shape[0]
    leaf_local = leaf_weight.shape[2]
    most = max(2, 4 * row_group // CLUSTERS)
    capacity = local_clusters * most
    my_cluster = lax.axis_index("cluster")
    my_row = lax.axis_index("rows")
    my_head = lax.axis_index("head")
    column_start = (my_row * heads_axis + my_head) * leaf_local
    valid = jnp.arange(cache_len)[None, :] < lengths[:, None]
    index = jnp.arange(row_group)
    slot_range = jnp.arange(capacity)
    results = []
    for step in range(STEPS):
        query = queries[step].reshape(own_rows, kv_local, group, head_dim)
        cached = (
            jnp.einsum("rkgd,rkpd->rkgp", query, key_cache, preferred_element_type=jnp.float32)
            * scale
        )
        cached = jnp.where(valid[:, None, None, :], cached, -jnp.inf)
        fresh_keys = new_keys[: step + 1].reshape(step + 1, own_rows, kv_local, head_dim)
        fresh_values = new_values[: step + 1].reshape(step + 1, own_rows, kv_local, head_dim)
        recent = (
            jnp.einsum("rkgd,srkd->rkgs", query, fresh_keys, preferred_element_type=jnp.float32)
            * scale
        )
        peak = jnp.maximum(jnp.max(cached, axis=-1), jnp.max(recent, axis=-1))
        e_cached = jnp.exp(cached - peak[..., None])
        e_recent = jnp.exp(recent - peak[..., None])
        total = jnp.sum(e_cached, axis=-1) + jnp.sum(e_recent, axis=-1)
        w_cached = (e_cached / total[..., None]).astype(jnp.bfloat16)
        w_recent = (e_recent / total[..., None]).astype(jnp.bfloat16)
        output = jnp.einsum(
            "rkgp,rkpd->rkgd", w_cached, value_cache, preferred_element_type=jnp.float32
        )
        output = output + jnp.einsum(
            "rkgs,srkd->rkgd", w_recent, fresh_values, preferred_element_type=jnp.float32
        )
        attended = output.astype(jnp.bfloat16).reshape(own_rows, kv_local * group * head_dim)
        partial_sum = jnp.dot(
            lax.all_gather(attended, "cluster", axis=0, tiled=True),
            out_weight,
            preferred_element_type=jnp.float32,
        )
        mixed = lax.psum(partial_sum, "head")
        residual_part = residual_in[step].astype(jnp.float32)
        hidden = mixed + residual_part
        squares = jnp.sum(hidden * hidden, axis=1)
        gated = (hidden * norm_gain).astype(jnp.bfloat16)
        top_partial = jnp.dot(gated, top_weight, preferred_element_type=jnp.float32)
        squares, top_logits = lax.psum((squares, top_partial), "cluster")
        inv_rms = lax.rsqrt(squares / D + 1e-05)
        top_logprob = jax.nn.log_softmax(top_logits * inv_rms[:, None], axis=-1)
        normed = (hidden * norm_gain * inv_rms[:, None]).astype(jnp.bfloat16)
        step_ids = cluster_ids[step, :, 0].reshape(row_groups, row_group)
        step_targets = targets[step].reshape(row_groups, row_group)
        earlier = (step_ids[:, :, None] == step_ids[:, None, :]) & (
            index[None, None, :] < index[None, :, None]
        )
        rank = jnp.sum(earlier.astype(jnp.int32), axis=2)
        dest = step_ids // local_clusters
        slot = step_ids % local_clusters * most + rank
        own_ids = lax.dynamic_index_in_dim(step_ids, my_row, 0, keepdims=False)
        own_dest = lax.dynamic_index_in_dim(dest, my_row, 0, keepdims=False)
        own_slot = lax.dynamic_index_in_dim(slot, my_row, 0, keepdims=False)
        top_pick = jnp.sum(
            jnp.where(jnp.arange(CLUSTERS)[None, :] == own_ids[:, None], top_logprob, 0.0), axis=1
        )
        sending = (own_dest[None, None, :] == jnp.arange(clusters_axis)[:, None, None]) & (
            own_slot[None, None, :] == slot_range[None, :, None]
        )
        outgoing = jnp.einsum(
            "dsi,if->sdf", sending.astype(jnp.bfloat16), normed, preferred_element_type=jnp.float32
        )
        outgoing = outgoing.astype(jnp.bfloat16).reshape(capacity, -1)
        arrived = lax.all_to_all(outgoing, "cluster", split_axis=1, concat_axis=1, tiled=True)
        both = lax.all_gather(arrived, "rows", axis=0, tiled=True).reshape(
            row_groups, local_clusters, most, D
        )
        logits = jnp.einsum("ncmd,cdv->ncmv", both, leaf_weight, preferred_element_type=jnp.float32)
        landing = (dest == my_cluster)[:, None, :] & (slot[:, None, :] == slot_range[None, :, None])
        slot_target = jnp.sum(jnp.where(landing, step_targets[:, None, :], 0), axis=2)
        target_here = slot_target.reshape(row_groups, local_clusters, most) - column_start
        hit = jnp.arange(leaf_local)[None, None, None, :] == target_here[..., None]
        picked = jnp.sum(jnp.where(hit, logits, 0.0), axis=-1)
        leaf_peak = jnp.max(logits, axis=-1)
        mass = jnp.sum(jnp.exp(logits - leaf_peak[..., None]), axis=-1)
        leaf_peak, mass, picked = merged(
            (leaf_peak, mass, picked), ("rows", "head"), combine_totals
        )
        leaf_logprob = (picked - leaf_peak - jnp.log(mass)).reshape(row_groups, capacity)
        own_logprob = lax.dynamic_index_in_dim(leaf_logprob, my_row, 0, keepdims=False)
        own_landing = lax.dynamic_index_in_dim(landing, my_row, 0, keepdims=False)
        spread = jnp.sum(jnp.where(own_landing, own_logprob[:, None], 0.0), axis=0)
        back = lax.psum_scatter(spread, "cluster", scatter_dimension=0, tiled=True)
        top_own = lax.dynamic_slice_in_dim(top_pick, my_cluster * own_rows, own_rows, 0)
        results.append(top_own + back)
    return jnp.stack(results, axis=0)


def solution(mesh):
    placed = (
        P(None, ("rows", "cluster"), "head"),
        P(None, ("rows", "cluster"), "head"),
        P(None, ("rows", "cluster"), "head"),
        P(("rows", "cluster"), "head", None, None),
        P(("rows", "cluster"), "head", None, None),
        P(("rows", "cluster")),
        P(None, "rows", "cluster"),
        P("head", "cluster"),
        P("cluster"),
        P("cluster", None),
        P("cluster", None, ("rows", "head")),
        P(),
        P(),
    )
    return jax.shard_map(
        shards, mesh=mesh, in_specs=placed, out_specs=P(None, ("rows", "cluster")), check_vma=False
    )
```

profile of v0, /device:TPU:2, one launch (start us, length us, event | category | flops | bytes accessed | tf_op | source)
XLA Modules:
  0.0 766.7 jit_solution(16518504707865597806)
XLA Ops:
  8.9 1.1 slice_bitcast_fusion.2
  10.3 2.3 fusion.147
  14.7 2.4 fusion.145
  19.1 2.4 fusion.144
  23.3 2.4 fusion.149
  28.6 30.9 %all-gather.29.cloned.1.call-done = bf16[256,2048]{1,0:T(8,128)(2,1)} async-done(((bf16[16,2048]{1,0:T(8,128)(2,1)}), bf16[256,2048]{1,0:T(8,128)(2,1)}) %all-gather.29.cloned.1.call-update) | async-done | bytes 1048592 | tf_op jit(solution)/shard_map/all_gather | solution.py:91
  59.5 2.7 fusion.158
  62.2 41.3 %all-gather.31.cloned.1.call-done = bf16[256,2048]{1,0:T(8,128)(2,1)} async-done(((bf16[16,2048]{1,0:T(8,128)(2,1)}), bf16[256,2048]{1,0:T(8,128)(2,1)}) %all-gather.31.cloned.1.call-update) | async-done | bytes 1048592 | tf_op jit(solution)/shard_map/all_gather | solution.py:91
  103.6 2.7 fusion.159
  106.3 41.3 %all-gather.25.cloned.1.call-done = bf16[256,2048]{1,0:T(8,128)(2,1)} async-done(((bf16[16,2048]{1,0:T(8,128)(2,1)}), bf16[256,2048]{1,0:T(8,128)(2,1)}) %all-gather.25.cloned.1.call-update) | async-done | bytes 1048592 | tf_op jit(solution)/shard_map/all_gather | solution.py:91
  147.6 2.7 fusion.156
  150.3 41.2 %all-gather.27.cloned.1.call-done = bf16[256,2048]{1,0:T(8,128)(2,1)} async-done(((bf16[16,2048]{1,0:T(8,128)(2,1)}), bf16[256,2048]{1,0:T(8,128)(2,1)}) %all-gather.27.cloned.1.call-update) | async-done | bytes 1048592 | tf_op jit(solution)/shard_map/all_gather | solution.py:91
  191.5 2.7 fusion.157
  195.0 56.2 %all-reduce.13.cloned.1.call-done = (f32[256,512]{1,0:T(8,128)}, f32[256,512]{1,0:T(8,128)}, f32[256,512]{1,0:T(8,128)}, f32[256,512]{1,0:T(8,128)}) async-done(((f32[256,512]{1,0:T(8,128)}, f32[256,512]{1,0:T(8,128)}, f32[256,512]{1,0:T(8,128)}, f32[256,512]{1,0:T(8,128)}), (f32[256,512]{1,0:T(8,128)}, f32[256,512]{1,0:T(8,128)}, f32[256,512]{1,0:T(8,128)}, ...) | async-done | bytes 2097168 | tf_op jit(solution)/shard_map/psum | solution.py:95
  251.2 1.9 multiply_reduce_fusion.3
  253.0 40.6 %all-reduce.5 = (f32[256]{0:T(256)S(1)}, f32[256]{0:T(256)S(1)}, f32[256]{0:T(256)S(1)}, f32[256]{0:T(256)S(1)}) all-reduce(f32[256]{0:T(256)S(1)} %get-tuple-element.899, f32[256]{0:T(256)S(1)} %get-tuple-element.900, f32[256]{0:T(256)S(1)} %get-tuple-element.901, ...), channel_id=1, replica_groups=mesh['rows'=2,'head'=4,'cluster'=16] {'cluster'}, use_global_device_ids=true, to_apply=%region_61.63 | all-reduce | flops 1024 | bytes 8192 | tf_op jit(solution)/shard_map/psum | solution.py:101
  293.6 1.9 fusion.64
  295.5 2.6 fusion.23
  298.1 3.7 all-to-all-start.3
  301.8 2.0 fusion.67
  303.8 2.0 fusion.66
  305.8 1.8 fusion.65
  307.7 6.9 all-to-all-done.3
  314.6 1.5 copy.425
  316.1 2.5 reshape.625
  318.7 2.5 fusion.22
  321.1 3.7 all-to-all-start.2
  325.1 12.7 %all-to-all-done.2 = bf16[60,16,512]{2,0,1:T(8,128)(2,1)S(1)} async-done(((bf16[60,16,512]{2,0,1:T(8,128)(2,1)}), bf16[60,16,512]{2,0,1:T(8,128)(2,1)S(1)}, u32[]{:S(2)}, u32[]{:S(2)}) %all-to-all-start.2) | async-done | bytes 983072 | tf_op jit(solution)/shard_map/all_to_all | solution.py:126
  337.8 1.5 copy.404
  339.3 2.4 reshape.623
  341.8 2.5 fusion.21
  344.2 3.7 all-to-all-start.1
  349.8 11.1 %all-to-all-done.1 = bf16[60,16,512]{2,0,1:T(8,128)(2,1)S(1)} async-done(((bf16[60,16,512]{2,0,1:T(8,128)(2,1)}), bf16[60,16,512]{2,0,1:T(8,128)(2,1)S(1)}, u32[]{:S(2)}, u32[]{:S(2)}) %all-to-all-start.1) | async-done | bytes 983072 | tf_op jit(solution)/shard_map/all_to_all | solution.py:126
  360.9 1.5 copy.383
  362.4 2.4 reshape.621
  364.9 2.5 fusion.20
  367.3 3.7 all-to-all-start
  371.0 33.0 %all-reduce.11.cloned.1.call-done = (f32[256,80]{0,1:T(8,128)}, f32[256,80]{0,1:T(8,128)}, f32[256,80]{0,1:T(8,128)}, f32[256,80]{0,1:T(8,128)}) async-done(((f32[256,80]{0,1:T(8,128)}, f32[256,80]{0,1:T(8,128)}, f32[256,80]{0,1:T(8,128)}, f32[256,80]{0,1:T(8,128)}), (f32[256,80]{0,1:T(8,128)}, f32[256,80]{0,1:T(8,128)}, f32[256,80]{0,1:T(8,128)}, f32[256,80]{0,1:T(8,128)})) %all-reduce.11.cloned.1.call-update) | async-done | bytes 327696 | tf_op jit(solution)/shard_map/psum | solution.py:101
  411.4 0.9 fusion.107
  413.3 0.9 fusion.105
  414.2 0.9 fusion.104
  415.2 1.5 copy.362
  416.7 2.3 reshape.619
  419.1 3.6 copy.426
  422.7 5.6 fusion.151
  428.6 21.7 %all-gather.10 = f32[16,5,12]{2,1,0:T(8,128)S(1)} all-gather(f32[2,5,12]{2,1,0:T(8,128)S(1)} %copy.429), channel_id=12, replica_groups=mesh['rows'=2,'head'=4,'cluster'=16] {'rows','head'}, dimensions={0}, use_global_device_ids=true | all-gather | bytes 4320 | tf_op jit(solution)/shard_map/all_gather | solution.py:12
  450.3 21.6 %all-gather.9 = f32[16,5,12]{2,1,0:T(8,128)S(1)} all-gather(f32[2,5,12]{2,1,0:T(8,128)S(1)} %copy.428), channel_id=11, replica_groups=mesh['rows'=2,'head'=4,'cluster'=16] {'rows','head'}, dimensions={0}, use_global_device_ids=true | all-gather | bytes 4320 | tf_op jit(solution)/shard_map/all_gather | solution.py:12
  471.9 21.7 %all-gather.11 = f32[16,5,12]{2,1,0:T(8,128)S(1)} all-gather(f32[2,5,12]{2,1,0:T(8,128)S(1)} %copy.433), channel_id=13, replica_groups=mesh['rows'=2,'head'=4,'cluster'=16] {'rows','head'}, dimensions={0}, use_global_device_ids=true | all-gather | bytes 4320 | tf_op jit(solution)/shard_map/all_gather | solution.py:12
  494.1 3.6 copy.405
  497.8 5.6 fusion.152
  503.6 21.5 %all-gather.7 = f32[16,5,12]{2,1,0:T(8,128)S(1)} all-gather(f32[2,5,12]{2,1,0:T(8,128)S(1)} %copy.408), channel_id=9, replica_groups=mesh['rows'=2,'head'=4,'cluster'=16] {'rows','head'}, dimensions={0}, use_global_device_ids=true | all-gather | bytes 4320 | tf_op jit(solution)/shard_map/all_gather | solution.py:12
  525.2 21.5 %all-gather.6 = f32[16,5,12]{2,1,0:T(8,128)S(1)} all-gather(f32[2,5,12]{2,1,0:T(8,128)S(1)} %copy.407), channel_id=8, replica_groups=mesh['rows'=2,'head'=4,'cluster'=16] {'rows','head'}, dimensions={0}, use_global_device_ids=true | all-gather | bytes 4320 | tf_op jit(solution)/shard_map/all_gather | solution.py:12
  546.7 21.5 %all-gather.8 = f32[16,5,12]{2,1,0:T(8,128)S(1)} all-gather(f32[2,5,12]{2,1,0:T(8,128)S(1)} %copy.412), channel_id=10, replica_groups=mesh['rows'=2,'head'=4,'cluster'=16] {'rows','head'}, dimensions={0}, use_global_device_ids=true | all-gather | bytes 4320 | tf_op jit(solution)/shard_map/all_gather | solution.py:12
  568.8 3.6 copy.384
  572.4 5.6 fusion.153
  578.3 21.5 %all-gather.4 = f32[16,5,12]{2,1,0:T(8,128)S(1)} all-gather(f32[2,5,12]{2,1,0:T(8,128)S(1)} %copy.387), channel_id=6, replica_groups=mesh['rows'=2,'head'=4,'cluster'=16] {'rows','head'}, dimensions={0}, use_global_device_ids=true | all-gather | bytes 4320 | tf_op jit(solution)/shard_map/all_gather | solution.py:12
  599.8 21.5 %all-gather.3 = f32[16,5,12]{2,1,0:T(8,128)S(1)} all-gather(f32[2,5,12]{2,1,0:T(8,128)S(1)} %copy.386), channel_id=5, replica_groups=mesh['rows'=2,'head'=4,'cluster'=16] {'rows','head'}, dimensions={0}, use_global_device_ids=true | all-gather | bytes 4320 | tf_op jit(solution)/shard_map/all_gather | solution.py:12
  621.4 21.8 %all-gather.5 = f32[16,5,12]{2,1,0:T(8,128)S(1)} all-gather(f32[2,5,12]{2,1,0:T(8,128)S(1)} %copy.391), channel_id=7, replica_groups=mesh['rows'=2,'head'=4,'cluster'=16] {'rows','head'}, dimensions={0}, use_global_device_ids=true | all-gather | bytes 4320 | tf_op jit(solution)/shard_map/all_gather | solution.py:12
  643.7 3.6 copy.363
  647.4 5.6 fusion.154
  653.2 21.5 %all-gather.1 = f32[16,5,12]{2,1,0:T(8,128)S(1)} all-gather(f32[2,5,12]{2,1,0:T(8,128)S(1)} %copy.366), channel_id=3, replica_groups=mesh['rows'=2,'head'=4,'cluster'=16] {'rows','head'}, dimensions={0}, use_global_device_ids=true | all-gather | bytes 4320 | tf_op jit(solution)/shard_map/all_gather | solution.py:12
  674.8 21.5 %all-gather = f32[16,5,12]{2,1,0:T(8,128)S(1)} all-gather(f32[2,5,12]{2,1,0:T(8,128)S(1)} %copy.365), channel_id=2, replica_groups=mesh['rows'=2,'head'=4,'cluster'=16] {'rows','head'}, dimensions={0}, use_global_device_ids=true | all-gather | bytes 4320 | tf_op jit(solution)/shard_map/all_gather | solution.py:12
  696.3 21.5 %all-gather.2 = f32[16,5,12]{2,1,0:T(8,128)S(1)} all-gather(f32[2,5,12]{2,1,0:T(8,128)S(1)} %copy.370), channel_id=4, replica_groups=mesh['rows'=2,'head'=4,'cluster'=16] {'rows','head'}, dimensions={0}, use_global_device_ids=true | all-gather | bytes 4320 | tf_op jit(solution)/shard_map/all_gather | solution.py:12
  718.8 40.1 %all-reduce.4 = (f32[256]{0:T(256)S(1)}, f32[256]{0:T(256)S(1)}, f32[256]{0:T(256)S(1)}, f32[256]{0:T(256)S(1)}) all-reduce(f32[256]{0:T(256)S(1)} %select_reduce_fusion.8, f32[256]{0:T(256)S(1)} %select_reduce_fusion.9, f32[256]{0:T(256)S(1)} %select_reduce_fusion.10, ...), channel_id=17, replica_groups=mesh['rows'=2,'head'=4,'cluster'=16] {'cluster'}, use_global_device_ids=true, to_apply=%region_71.73.clone | all-reduce | flops 1024 | bytes 8192
  (292 shorter events, 27.1 us)
Async XLA Ops:
  6.5 53.0 %copy-start = (bf16[2048,512]{1,0:T(8,128)(2,1)S(1)}, bf16[2048,512]{1,0:T(8,128)(2,1)}, u32[]{:S(2)}) copy-start(bf16[2048,512]{1,0:T(8,128)(2,1)} %param.29) | copy-start | bytes 6291460
  6.5 53.0 %all-gather.29.cloned.1.call-start = ((), (), s32[]{:S(2)}) async-start(), calls=%async_computation.6 | async-start | bytes 1114112 | tf_op jit(solution)/shard_map/all_gather | solution.py:91
  8.9 4.3 copy-start.12
  12.7 1.7 copy-start.7
  12.9 1.5 copy-start.8
  14.3 89.2 %all-gather.31.cloned.1.call-start = ((), (), s32[]{:S(2)}) async-start(), calls=%async_computation.7 | async-start | bytes 1114112 | tf_op jit(solution)/shard_map/all_gather | solution.py:91
  14.4 3.3 copy-start.13
  17.2 1.7 slice-start
  18.8 128.8 %all-gather.25.cloned.1.call-start = ((), (), s32[]{:S(2)}) async-start(), calls=%async_computation.4 | async-start | bytes 1114112 | tf_op jit(solution)/shard_map/all_gather | solution.py:91
  18.9 2.9 copy-start.14
  21.6 1.5 slice-start.1
  21.6 1.5 slice-start.2
  23.0 168.5 %all-gather.27.cloned.1.call-start = ((), (), s32[]{:S(2)}) async-start(), calls=%async_computation.5 | async-start | bytes 1114112 | tf_op jit(solution)/shard_map/all_gather | solution.py:91
  23.1 3.3 copy-start.15
  25.9 1.7 copy-start.10
  26.1 1.5 copy-start.11
  27.5 223.7 %all-reduce.13.cloned.1.call-start = ((), (), s32[]{:S(2)}) async-start(), calls=%async_computation.13 | async-start | bytes 4194304 | tf_op jit(solution)/shard_map/psum | solution.py:95
  150.3 100.8 %copy-start.1 = (bf16[4,256,512]{2,1,0:T(8,128)(2,1)S(1)}, bf16[4,256,512]{2,1,0:T(8,128)(2,1)}, u32[]{:S(2)}) copy-start(bf16[4,256,512]{2,1,0:T(8,128)(2,1)} %param.28) | copy-start | bytes 3145732
  194.3 99.3 %copy-start.6 = (bf16[512,80]{0,1:T(8,128)(2,1)S(1)}, bf16[512,80]{0,1:T(8,128)(2,1)}, u32[]{:S(2)}) copy-start(bf16[512,80]{0,1:T(8,128)(2,1)} %param.31) | copy-start | bytes 245764
  194.3 99.3 %copy-start.9 = (f32[512]{0:T(512)S(1)}, f32[512]{0:T(512)}, u32[]{:S(2)}) copy-start(f32[512]{0:T(512)} %param.30) | copy-start | bytes 6148
  298.1 16.5 %all-to-all-start.3 = ((bf16[60,16,512]{2,0,1:T(8,128)(2,1)}), bf16[60,16,512]{2,0,1:T(8,128)(2,1)S(1)}, u32[]{:S(2)}, u32[]{:S(2)}) async-start(bf16[60,16,512]{2,0,1:T(8,128)(2,1)} %fusion.23), calls=%async_computation.3 | async-start | bytes 2097152 | tf_op jit(solution)/shard_map/all_to_all | solution.py:126
  301.7 102.3 %all-reduce.11.cloned.1.call-start = ((), (), s32[]{:S(2)}) async-start(), calls=%async_computation.12 | async-start | bytes 655360 | tf_op jit(solution)/shard_map/psum | solution.py:101
  301.8 4.0 copy-start.3
  307.6 111.5 %all-gather.39.cloned.1.call-start = ((), (), s32[]{:S(2)}) async-start(), calls=%async_computation.11 | async-start | bytes 3145728 | tf_op jit(solution)/shard_map/all_gather | solution.py:127
  316.1 2.6 copy-start.5
  321.1 16.6 %all-to-all-start.2 = ((bf16[60,16,512]{2,0,1:T(8,128)(2,1)}), bf16[60,16,512]{2,0,1:T(8,128)(2,1)S(1)}, u32[]{:S(2)}, u32[]{:S(2)}) async-start(bf16[60,16,512]{2,0,1:T(8,128)(2,1)} %fusion.22), calls=%async_computation.2 | async-start | bytes 2097152 | tf_op jit(solution)/shard_map/all_to_all | solution.py:126
  324.8 169.3 %all-gather.37.cloned.1.call-start = ((), (), s32[]{:S(2)}) async-start(), calls=%async_computation.10 | async-start | bytes 3145728 | tf_op jit(solution)/shard_map/all_gather | solution.py:127
  339.3 2.5 copy-start.4
  341.8 6.5 copy-start.16
  344.2 16.7 %all-to-all-start.1 = ((bf16[60,16,512]{2,0,1:T(8,128)(2,1)}), bf16[60,16,512]{2,0,1:T(8,128)(2,1)S(1)}, u32[]{:S(2)}, u32[]{:S(2)}) async-start(bf16[60,16,512]{2,0,1:T(8,128)(2,1)} %fusion.21), calls=%async_computation.1 | async-start | bytes 2097152 | tf_op jit(solution)/shard_map/all_to_all | solution.py:126
  347.9 220.9 %all-gather.35.cloned.1.call-start = ((), (), s32[]{:S(2)}) async-start(), calls=%async_computation.9 | async-start | bytes 3145728 | tf_op jit(solution)/shard_map/all_gather | solution.py:127
  362.4 2.5 copy-start.2
  367.3 47.8 %all-to-all-start = ((bf16[60,16,512]{2,0,1:T(8,128)(2,1)}), bf16[60,16,512]{2,0,1:T(8,128)(2,1)S(1)}, u32[]{:S(2)}, u32[]{:S(2)}) async-start(bf16[60,16,512]{2,0,1:T(8,128)(2,1)} %fusion.20), calls=%async_computation | async-start | bytes 2097152 | tf_op jit(solution)/shard_map/all_to_all | solution.py:126
  371.0 272.7 %all-gather.33.cloned.1.call-start = ((), (), s32[]{:S(2)}) async-start(), calls=%async_computation.8 | async-start | bytes 3145728 | tf_op jit(solution)/shard_map/all_gather | solution.py:127
Sparse Core Ops, SparseCore 0:
  14.5 45.0 all-gather.28
  61.6 41.8 all-gather.30
  105.7 41.8 all-gather.24
  149.6 41.8 all-gather.26
  194.4 56.7 all-reduce.12
  307.7 96.2 all-reduce.10
  405.7 12.7 all-gather.38
  420.1 14.6 all-gather.36
  436.4 14.6 all-gather.34
  452.5 14.6 all-gather.32
where the time goes:
time: 769 us; the launch traced here: 767 us
  blocking collectives  340 us (44%)
  waiting for transfers between devices  275 us (36%)
  matrix products  63.8 us (8%)
  local copies, waits for them, and re-layouts  37.6 us (5%)
  other arithmetic  19.9 us (3%)
  between operations  15.3 us (2%)
  starting transfers between devices  15.2 us (2%)
    all_gather x12, blocking collectives, merged(): gathered = jax.tree.map(lambda a: lax.all_gather(a, axis), part)  259 us
    all_gather x4, waiting for transfers between devices, shards(): lax.all_gather(attended, 'cluster', axis=0, tiled=True)  155 us
    psum x1, waiting for transfers between devices, shards(): mixed = lax.psum(partial_sum, 'head')  56.2 us
    psum x1, blocking collectives, shards(): squares, top_logits = lax.psum((squares, top_partial), 'cluster')  40.6 us
    unnamed x1, blocking collectives  40.1 us
    psum x1, waiting for transfers between devices, shards(): squares, top_logits = lax.psum((squares, top_partial), 'cluster')  33 us
    all_to_all x4, waiting for transfers between devices, shards(): lax.all_to_all(outgoing, 'cluster', split_axis=1, concat_axis=1, tiled=True)  30.7 us
    dot_general x4, matrix products, shards(): jnp.einsum('ncmd,cdv->ncmv', both, leaf_weight, preferred_element_type=jn...  22.4 us
  transfers between devices with their start and end apart: 14, of which 9 were waited for; matrix products, arithmetic and copies ran while one was open for 12% of the time, Pallas kernels for 0%

commit v1 on v0

--- a/solution.py
+++ b/solution.py
@@ -6,6 +6,27 @@
 D = 8192
 CLUSTERS = 80
 STEPS = 4
+
+
+def ring_gather(shard, axis, dim):
+    size, index, width = (lax.axis_size(axis), lax.axis_index(axis), shard.shape[dim])
+    right = [(i, (i + 1) % size) for i in range(size)]
+    behind = [(i, (i - 1) % size) for i in range(size)]
+    out = jnp.zeros((*shard.shape[:dim], size * width, *shard.shape[dim + 1 :]), shard.dtype)
+    out = lax.dynamic_update_slice_in_dim(out, shard, index * width, axis=dim)
+    from_left = from_right = shard
+    halfway = size // 2
+    for turn in range(1, halfway + 1):
+        from_left = lax.ppermute(from_left, axis, right)
+        out = lax.dynamic_update_slice_in_dim(
+            out, from_left, (index - turn) % size * width, axis=dim
+        )
+        if turn < size - halfway:
+            from_right = lax.ppermute(from_right, axis, behind)
+            out = lax.dynamic_update_slice_in_dim(
+                out, from_right, (index + turn) % size * width, axis=dim
+            )
+    return out
 
 
 def merged(part, axis, combine):
@@ -88,9 +109,7 @@
         )
         attended = output.astype(jnp.bfloat16).reshape(own_rows, kv_local * group * head_dim)
         partial_sum = jnp.dot(
-            lax.all_gather(attended, "cluster", axis=0, tiled=True),
-            out_weight,
-            preferred_element_type=jnp.float32,
+            ring_gather(attended, "cluster", 0), out_weight, preferred_element_type=jnp.float32
         )
         mixed = lax.psum(partial_sum, "head")
         residual_part = residual_in[step].astype(jnp.float32)

time: 769 us -> 809 us (1.052)
  starting transfers between devices: 15.2 us -> 167 us
  waiting for transfers between devices: 275 us -> 131 us
  local copies, waits for them, and re-layouts: 37.6 us -> 64.4 us
    all_gather x4 -> x0, waiting for transfers between devices: 155 us -> none  [shards(): lax.all_gather(attended, 'cluster', axis=0, tiled=True)]
    ppermute x0 -> x60, starting transfers between devices: none -> 152 us  [the longest x28 149 us: ring_gather(): from_right = lax.ppermute(from_right, axis, behind)]
    dynamic_update_slice x0 -> x64, local copies, waits for them, and re-layouts: none -> 31.9 us  [the longest x32 16.3 us: ring_gather(): lax.dynamic_update_slice_in_dim(out, from_left, (index - turn) % size * w...]
  transfers between devices with their start and end apart: 14 -> 70, of which waited for: 9 -> 8; matrix products, arithmetic and copies ran while one was open for 12% -> 14% of each run, Pallas kernels for 0% -> 0%
where the time goes in v1:
time: 809 us; the launch traced here: 799 us
  blocking collectives  340 us (42%)
  starting transfers between devices  167 us (21%)
  waiting for transfers between devices  131 us (16%)
  local copies, waits for them, and re-layouts  64.4 us (8%)
  matrix products  57.9 us (7%)
  other arithmetic  21 us (3%)
  between operations  15.9 us (2%)
    all_gather x12, blocking collectives, merged(): gathered = jax.tree.map(lambda a: lax.all_gather(a, axis), part)  259 us
    ppermute x28, starting transfers between devices, ring_gather(): from_right = lax.ppermute(from_right, axis, behind)  149 us
    psum x1, waiting for transfers between devices, shards(): mixed = lax.psum(partial_sum, 'head')  55.5 us
    psum x1, blocking collectives, shards(): squares, top_logits = lax.psum((squares, top_partial), 'cluster')  40.6 us
    unnamed x1, blocking collectives  40.6 us
    psum x1, waiting for transfers between devices, shards(): squares, top_logits = lax.psum((squares, top_partial), 'cluster')  37 us
    all_to_all x4, waiting for transfers between devices, shards(): lax.all_to_all(outgoing, 'cluster', split_axis=1, concat_axis=1, tiled=True)  32.9 us
    dot_general x4, matrix products, shards(): jnp.einsum('ncmd,cdv->ncmv', both, leaf_weight, preferred_element_type=jn...  22.3 us
  transfers between devices with their start and end apart: 70, of which 8 were waited for; matrix products, arithmetic and copies ran while one was open for 14% of the time, Pallas kernels for 0%

profile of v1, /device:TPU:2, one launch (start us, length us, event | category | flops | bytes accessed | tf_op | source)
XLA Modules:
  0.0 798.7 jit_solution(9253531012051287498)
XLA Ops:
  17.6 4.6 collective-permute-start.16
  26.5 5.3 collective-permute-start.31
  46.1 5.4 collective-permute-start.46
  53.9 5.3 collective-permute-start.1
  61.6 5.3 collective-permute-start.18
  69.1 5.3 collective-permute-start.33
  75.7 5.3 collective-permute-start.48
  81.9 5.3 collective-permute-start.3
  88.0 5.3 collective-permute-start.20
  94.6 5.3 collective-permute-start.35
  101.2 5.3 collective-permute-start.50
  107.3 5.3 collective-permute-start.5
  113.3 5.3 collective-permute-start.22
  119.9 5.3 collective-permute-start.37
  126.5 5.3 collective-permute-start.52
  132.6 5.3 collective-permute-start.7
  138.6 5.3 collective-permute-start.24
  145.2 5.3 collective-permute-start.39
  151.8 5.3 collective-permute-start.54
  157.9 5.3 collective-permute-start.9
  164.0 5.3 collective-permute-start.26
  170.5 5.3 collective-permute-start.41
  177.1 5.5 collective-permute-start.56
  183.4 5.3 collective-permute-start.11
  189.5 5.3 collective-permute-start.28
  196.1 5.4 collective-permute-start.43
  202.7 5.3 collective-permute-start.58
  208.7 5.3 collective-permute-start.13
  217.6 4.2 collective-permute-done.29
  226.9 2.8 fusion.156
  230.5 55.5 %all-reduce.13.cloned.1.call-done = (f32[256,512]{1,0:T(8,128)}, f32[256,512]{1,0:T(8,128)}, f32[256,512]{1,0:T(8,128)}, f32[256,512]{1,0:T(8,128)}) async-done(((f32[256,512]{1,0:T(8,128)}, f32[256,512]{1,0:T(8,128)}, f32[256,512]{1,0:T(8,128)}, f32[256,512]{1,0:T(8,128)}), (f32[256,512]{1,0:T(8,128)}, f32[256,512]{1,0:T(8,128)}, f32[256,512]{1,0:T(8,128)}, ...) | async-done | bytes 2097168 | tf_op jit(solution)/shard_map/psum | solution.py:114
  287.9 40.6 %all-reduce.5 = (f32[256]{0:T(256)S(1)}, f32[256]{0:T(256)S(1)}, f32[256]{0:T(256)S(1)}, f32[256]{0:T(256)S(1)}) all-reduce(f32[256]{0:T(256)S(1)} %get-tuple-element.899, f32[256]{0:T(256)S(1)} %get-tuple-element.900, f32[256]{0:T(256)S(1)} %get-tuple-element.901, ...), channel_id=1, replica_groups=mesh['rows'=2,'head'=4,'cluster'=16] {'cluster'}, use_global_device_ids=true, to_apply=%region_61.63 | all-reduce | flops 1024 | bytes 8192 | tf_op jit(solution)/shard_map/psum | solution.py:120
  330.9 3.8 all-to-all-start
  338.5 9.1 %all-to-all-done = bf16[60,16,512]{2,0,1:T(8,128)(2,1)S(1)} async-done(((bf16[60,16,512]{2,0,1:T(8,128)(2,1)}), bf16[60,16,512]{2,0,1:T(8,128)(2,1)S(1)}, u32[]{:S(2)}, u32[]{:S(2)}) %all-to-all-start) | async-done | bytes 983072 | tf_op jit(solution)/shard_map/all_to_all | solution.py:145
  349.7 2.6 fusion.21
  352.3 3.7 all-to-all-start.1
  356.5 12.4 %all-to-all-done.1 = bf16[60,16,512]{2,0,1:T(8,128)(2,1)S(1)} async-done(((bf16[60,16,512]{2,0,1:T(8,128)(2,1)}), bf16[60,16,512]{2,0,1:T(8,128)(2,1)S(1)}, u32[]{:S(2)}, u32[]{:S(2)}) %all-to-all-start.1) | async-done | bytes 983072 | tf_op jit(solution)/shard_map/all_to_all | solution.py:145
  371.0 2.6 fusion.22
  373.7 3.7 all-to-all-start.2
  379.1 11.4 %all-to-all-done.2 = bf16[60,16,512]{2,0,1:T(8,128)(2,1)S(1)} async-done(((bf16[60,16,512]{2,0,1:T(8,128)(2,1)}), bf16[60,16,512]{2,0,1:T(8,128)(2,1)S(1)}, u32[]{:S(2)}, u32[]{:S(2)}) %all-to-all-start.2) | async-done | bytes 983072 | tf_op jit(solution)/shard_map/all_to_all | solution.py:145
  392.5 2.6 fusion.23
  395.2 3.7 all-to-all-start.3
  398.9 37.0 %all-reduce.11.cloned.1.call-done = (f32[256,80]{0,1:T(8,128)}, f32[256,80]{0,1:T(8,128)}, f32[256,80]{0,1:T(8,128)}, f32[256,80]{0,1:T(8,128)}) async-done(((f32[256,80]{0,1:T(8,128)}, f32[256,80]{0,1:T(8,128)}, f32[256,80]{0,1:T(8,128)}, f32[256,80]{0,1:T(8,128)}), (f32[256,80]{0,1:T(8,128)}, f32[256,80]{0,1:T(8,128)}, f32[256,80]{0,1:T(8,128)}, f32[256,80]{0,1:T(8,128)})) %all-reduce.11.cloned.1.call-update) | async-done | bytes 327696 | tf_op jit(solution)/shard_map/psum | solution.py:120
  450.3 3.6 copy.363
  454.0 5.5 fusion.154
  459.7 21.9 %all-gather.1 = f32[16,5,12]{2,1,0:T(8,128)S(1)} all-gather(f32[2,5,12]{2,1,0:T(8,128)S(1)} %copy.366), channel_id=3, replica_groups=mesh['rows'=2,'head'=4,'cluster'=16] {'rows','head'}, dimensions={0}, use_global_device_ids=true | all-gather | bytes 4320 | tf_op jit(solution)/shard_map/all_gather | solution.py:33
  481.7 21.5 %all-gather.2 = f32[16,5,12]{2,1,0:T(8,128)S(1)} all-gather(f32[2,5,12]{2,1,0:T(8,128)S(1)} %copy.370), channel_id=4, replica_groups=mesh['rows'=2,'head'=4,'cluster'=16] {'rows','head'}, dimensions={0}, use_global_device_ids=true | all-gather | bytes 4320 | tf_op jit(solution)/shard_map/all_gather | solution.py:33
  503.3 21.7 %all-gather = f32[16,5,12]{2,1,0:T(8,128)S(1)} all-gather(f32[2,5,12]{2,1,0:T(8,128)S(1)} %copy.365), channel_id=2, replica_groups=mesh['rows'=2,'head'=4,'cluster'=16] {'rows','head'}, dimensions={0}, use_global_device_ids=true | all-gather | bytes 4320 | tf_op jit(solution)/shard_map/all_gather | solution.py:33
  525.5 3.6 copy.384
  529.1 5.5 fusion.153
  534.9 21.5 %all-gather.4 = f32[16,5,12]{2,1,0:T(8,128)S(1)} all-gather(f32[2,5,12]{2,1,0:T(8,128)S(1)} %copy.387), channel_id=6, replica_groups=mesh['rows'=2,'head'=4,'cluster'=16] {'rows','head'}, dimensions={0}, use_global_device_ids=true | all-gather | bytes 4320 | tf_op jit(solution)/shard_map/all_gather | solution.py:33
  556.5 21.5 %all-gather.5 = f32[16,5,12]{2,1,0:T(8,128)S(1)} all-gather(f32[2,5,12]{2,1,0:T(8,128)S(1)} %copy.391), channel_id=7, replica_groups=mesh['rows'=2,'head'=4,'cluster'=16] {'rows','head'}, dimensions={0}, use_global_device_ids=true | all-gather | bytes 4320 | tf_op jit(solution)/shard_map/all_gather | solution.py:33
  578.0 21.5 %all-gather.3 = f32[16,5,12]{2,1,0:T(8,128)S(1)} all-gather(f32[2,5,12]{2,1,0:T(8,128)S(1)} %copy.386), channel_id=5, replica_groups=mesh['rows'=2,'head'=4,'cluster'=16] {'rows','head'}, dimensions={0}, use_global_device_ids=true | all-gather | bytes 4320 | tf_op jit(solution)/shard_map/all_gather | solution.py:33
  600.1 3.6 copy.405
  603.7 5.5 fusion.152
  609.5 21.5 %all-gather.7 = f32[16,5,12]{2,1,0:T(8,128)S(1)} all-gather(f32[2,5,12]{2,1,0:T(8,128)S(1)} %copy.408), channel_id=9, replica_groups=mesh['rows'=2,'head'=4,'cluster'=16] {'rows','head'}, dimensions={0}, use_global_device_ids=true | all-gather | bytes 4320 | tf_op jit(solution)/shard_map/all_gather | solution.py:33
  631.0 21.5 %all-gather.8 = f32[16,5,12]{2,1,0:T(8,128)S(1)} all-gather(f32[2,5,12]{2,1,0:T(8,128)S(1)} %copy.412), channel_id=10, replica_groups=mesh['rows'=2,'head'=4,'cluster'=16] {'rows','head'}, dimensions={0}, use_global_device_ids=true | all-gather | bytes 4320 | tf_op jit(solution)/shard_map/all_gather | solution.py:33
  652.6 21.7 %all-gather.6 = f32[16,5,12]{2,1,0:T(8,128)S(1)} all-gather(f32[2,5,12]{2,1,0:T(8,128)S(1)} %copy.407), channel_id=8, replica_groups=mesh['rows'=2,'head'=4,'cluster'=16] {'rows','head'}, dimensions={0}, use_global_device_ids=true | all-gather | bytes 4320 | tf_op jit(solution)/shard_map/all_gather | solution.py:33
  674.9 3.6 copy.426
  678.5 5.7 fusion.151
  684.5 21.5 %all-gather.10 = f32[16,5,12]{2,1,0:T(8,128)S(1)} all-gather(f32[2,5,12]{2,1,0:T(8,128)S(1)} %copy.429), channel_id=12, replica_groups=mesh['rows'=2,'head'=4,'cluster'=16] {'rows','head'}, dimensions={0}, use_global_device_ids=true | all-gather | bytes 4320 | tf_op jit(solution)/shard_map/all_gather | solution.py:33
  706.1 21.5 %all-gather.11 = f32[16,5,12]{2,1,0:T(8,128)S(1)} all-gather(f32[2,5,12]{2,1,0:T(8,128)S(1)} %copy.433), channel_id=13, replica_groups=mesh['rows'=2,'head'=4,'cluster'=16] {'rows','head'}, dimensions={0}, use_global_device_ids=true | all-gather | bytes 4320 | tf_op jit(solution)/shard_map/all_gather | solution.py:33
  727.6 21.5 %all-gather.9 = f32[16,5,12]{2,1,0:T(8,128)S(1)} all-gather(f32[2,5,12]{2,1,0:T(8,128)S(1)} %copy.428), channel_id=11, replica_groups=mesh['rows'=2,'head'=4,'cluster'=16] {'rows','head'}, dimensions={0}, use_global_device_ids=true | all-gather | bytes 4320 | tf_op jit(solution)/shard_map/all_gather | solution.py:33
  750.1 40.6 %all-reduce.4 = (f32[256]{0:T(256)S(1)}, f32[256]{0:T(256)S(1)}, f32[256]{0:T(256)S(1)}, f32[256]{0:T(256)S(1)}) all-reduce(f32[256]{0:T(256)S(1)} %select_reduce_fusion.8, f32[256]{0:T(256)S(1)} %select_reduce_fusion.9, f32[256]{0:T(256)S(1)} %select_reduce_fusion.10, ...), channel_id=17, replica_groups=mesh['rows'=2,'head'=4,'cluster'=16] {'cluster'}, use_global_device_ids=true, to_apply=%region_71.73.clone | all-reduce | flops 1024 | bytes 8192
  (481 shorter events, 102.8 us)
Async XLA Ops:
  6.5 279.5 %all-reduce.13.cloned.1.call-start = ((), (), s32[]{:S(2)}) async-start(), calls=%async_computation.9 | async-start | bytes 4194304 | tf_op jit(solution)/shard_map/psum | solution.py:114
  15.7 30.4 %collective-permute-start.15 = (bf16[16,2048]{1,0:T(8,128)(2,1)}, bf16[16,2048]{1,0:T(8,128)(2,1)}, u32[]{:S(2)}, u32[]{:S(2)}) collective-permute-start(bf16[16,2048]{1,0:T(8,128)(2,1)} %bitcast.285), channel_id=1, source_target_pairs={{0,1},{1,2},{2,3},{3,4},{4,5},{5,6},{6,7},{7,8},{8,9},{9,10},{10,1... | collective-permute-start | bytes 196616 | tf_op jit(solution)/shard_map/ppermute | solution.py:20
  17.6 36.3 %collective-permute-start.16 = (bf16[16,2048]{1,0:T(8,128)(2,1)}, bf16[16,2048]{1,0:T(8,128)(2,1)}, u32[]{:S(2)}, u32[]{:S(2)}) collective-permute-start(bf16[16,2048]{1,0:T(8,128)(2,1)} %bitcast.285), channel_id=1, source_target_pairs={{0,15},{1,0},{2,1},{3,2},{4,3},{5,4},{6,5},{7,6},{8,7},{9,8},{10,9... | collective-permute-start | bytes 196616 | tf_op jit(solution)/shard_map/ppermute | solution.py:25
  26.5 25.9 %collective-permute-start.30 = (bf16[16,2048]{1,0:T(8,128)(2,1)}, bf16[16,2048]{1,0:T(8,128)(2,1)}, u32[]{:S(2)}, u32[]{:S(2)}) collective-permute-start(bf16[16,2048]{1,0:T(8,128)(2,1)} %bitcast.284), channel_id=1, source_target_pairs={{0,1},{1,2},{2,3},{3,4},{4,5},{5,6},{6,7},{7,8},{8,9},{9,10},{10,1... | collective-permute-start | bytes 196616 | tf_op jit(solution)/shard_map/ppermute | solution.py:20
  26.5 33.6 %collective-permute-start.31 = (bf16[16,2048]{1,0:T(8,128)(2,1)}, bf16[16,2048]{1,0:T(8,128)(2,1)}, u32[]{:S(2)}, u32[]{:S(2)}) collective-permute-start(bf16[16,2048]{1,0:T(8,128)(2,1)} %bitcast.284), channel_id=1, source_target_pairs={{0,15},{1,0},{2,1},{3,2},{4,3},{5,4},{6,5},{7,6},{8,7},{9,8},{10,9... | collective-permute-start | bytes 196616 | tf_op jit(solution)/shard_map/ppermute | solution.py:25
  36.3 25.4 %collective-permute-start.45 = (bf16[16,2048]{1,0:T(8,128)(2,1)}, bf16[16,2048]{1,0:T(8,128)(2,1)}, u32[]{:S(2)}, u32[]{:S(2)}) collective-permute-start(bf16[16,2048]{1,0:T(8,128)(2,1)} %bitcast.283), channel_id=1, source_target_pairs={{0,1},{1,2},{2,3},{3,4},{4,5},{5,6},{6,7},{7,8},{8,9},{9,10},{10,1... | collective-permute-start | bytes 196616 | tf_op jit(solution)/shard_map/ppermute | solution.py:20
  46.1 22.3 %collective-permute-start.46 = (bf16[16,2048]{1,0:T(8,128)(2,1)}, bf16[16,2048]{1,0:T(8,128)(2,1)S(1)}, u32[]{:S(2)}, u32[]{:S(2)}) collective-permute-start(bf16[16,2048]{1,0:T(8,128)(2,1)} %bitcast.283), channel_id=1, source_target_pairs={{0,15},{1,0},{2,1},{3,2},{4,3},{5,4},{6,5},{7,6},{8,7},{9,8},{10,9... | collective-permute-start | bytes 196616 | tf_op jit(solution)/shard_map/ppermute | solution.py:25
  52.4 16.7 %collective-permute-start = (bf16[16,2048]{1,0:T(8,128)(2,1)S(1)}, bf16[16,2048]{1,0:T(8,128)(2,1)S(1)}, u32[]{:S(2)}, u32[]{:S(2)}) collective-permute-start(bf16[16,2048]{1,0:T(8,128)(2,1)S(1)} %bitcast.329), channel_id=1, source_target_pairs={{0,1},{1,2},{2,3},{3,4},{4,5},{5,6},{6,7},{7,8},{8,9},{9,10},{10,1... | collective-permute-start | bytes 196616 | tf_op jit(solution)/shard_map/ppermute | solution.py:20
  53.9 21.1 %collective-permute-start.1 = (bf16[16,2048]{1,0:T(8,128)(2,1)S(1)}, bf16[16,2048]{1,0:T(8,128)(2,1)S(1)}, u32[]{:S(2)}, u32[]{:S(2)}) collective-permute-start(bf16[16,2048]{1,0:T(8,128)(2,1)S(1)} %bitcast.330), channel_id=1, source_target_pairs={{0,15},{1,0},{2,1},{3,2},{4,3},{5,4},{6,5},{7,6},{8,7},{9,8},{10,9... | collective-permute-start | bytes 196616 | tf_op jit(solution)/shard_map/ppermute | solution.py:25
  60.1 15.6 %collective-permute-start.17 = (bf16[16,2048]{1,0:T(8,128)(2,1)}, bf16[16,2048]{1,0:T(8,128)(2,1)S(1)}, u32[]{:S(2)}, u32[]{:S(2)}) collective-permute-start(bf16[16,2048]{1,0:T(8,128)(2,1)} %collective-permute-done.15), channel_id=1, source_target_pairs={{0,1},{1,2},{2,3},{3,4},{4,5},{5,6},{6,7},{7,8},{8,9},{9,10},{10,1... | collective-permute-start | bytes 196616 | tf_op jit(solution)/shard_map/ppermute | solution.py:20
  61.6 20.3 %collective-permute-start.18 = (bf16[16,2048]{1,0:T(8,128)(2,1)}, bf16[16,2048]{1,0:T(8,128)(2,1)S(1)}, u32[]{:S(2)}, u32[]{:S(2)}) collective-permute-start(bf16[16,2048]{1,0:T(8,128)(2,1)} %collective-permute-done.16), channel_id=1, source_target_pairs={{0,15},{1,0},{2,1},{3,2},{4,3},{5,4},{6,5},{7,6},{8,7},{9,8},{10,9... | collective-permute-start | bytes 196616 | tf_op jit(solution)/shard_map/ppermute | solution.py:25
  68.5 12.6 %collective-permute-start.32 = (bf16[16,2048]{1,0:T(8,128)(2,1)}, bf16[16,2048]{1,0:T(8,128)(2,1)S(1)}, u32[]{:S(2)}, u32[]{:S(2)}) collective-permute-start(bf16[16,2048]{1,0:T(8,128)(2,1)} %collective-permute-done.30), channel_id=1, source_target_pairs={{0,1},{1,2},{2,3},{3,4},{4,5},{5,6},{6,7},{7,8},{8,9},{9,10},{10,1... | collective-permute-start | bytes 196616 | tf_op jit(solution)/shard_map/ppermute | solution.py:20
  69.1 18.2 %collective-permute-start.33 = (bf16[16,2048]{1,0:T(8,128)(2,1)}, bf16[16,2048]{1,0:T(8,128)(2,1)S(1)}, u32[]{:S(2)}, u32[]{:S(2)}) collective-permute-start(bf16[16,2048]{1,0:T(8,128)(2,1)} %collective-permute-done.31), channel_id=1, source_target_pairs={{0,15},{1,0},{2,1},{3,2},{4,3},{5,4},{6,5},{7,6},{8,7},{9,8},{10,9... | collective-permute-start | bytes 196616 | tf_op jit(solution)/shard_map/ppermute | solution.py:25
  75.0 12.9 %collective-permute-start.47 = (bf16[16,2048]{1,0:T(8,128)(2,1)}, bf16[16,2048]{1,0:T(8,128)(2,1)S(1)}, u32[]{:S(2)}, u32[]{:S(2)}) collective-permute-start(bf16[16,2048]{1,0:T(8,128)(2,1)} %collective-permute-done.45), channel_id=1, source_target_pairs={{0,1},{1,2},{2,3},{3,4},{4,5},{5,6},{6,7},{7,8},{8,9},{9,10},{10,1... | collective-permute-start | bytes 196616 | tf_op jit(solution)/shard_map/ppermute | solution.py:20
  75.7 18.3 %collective-permute-start.48 = (bf16[16,2048]{1,0:T(8,128)(2,1)S(1)}, bf16[16,2048]{1,0:T(8,128)(2,1)S(1)}, u32[]{:S(2)}, u32[]{:S(2)}) collective-permute-start(bf16[16,2048]{1,0:T(8,128)(2,1)S(1)} %collective-permute-done.46), channel_id=1, source_target_pairs={{0,15},{1,0},{2,1},{3,2},{4,3},{5,4},{6,5},{7,6},{8,7},{9,8},{10,9... | collective-permute-start | bytes 196616 | tf_op jit(solution)/shard_map/ppermute | solution.py:25
  81.0 13.5 %collective-permute-start.2 = (bf16[16,2048]{1,0:T(8,128)(2,1)S(1)}, bf16[16,2048]{1,0:T(8,128)(2,1)S(1)}, u32[]{:S(2)}, u32[]{:S(2)}) collective-permute-start(bf16[16,2048]{1,0:T(8,128)(2,1)S(1)} %collective-permute-done), channel_id=1, source_target_pairs={{0,1},{1,2},{2,3},{3,4},{4,5},{5,6},{6,7},{7,8},{8,9},{9,10},{10,1... | collective-permute-start | bytes 196616 | tf_op jit(solution)/shard_map/ppermute | solution.py:20
  81.9 18.6 %collective-permute-start.3 = (bf16[16,2048]{1,0:T(8,128)(2,1)S(1)}, bf16[16,2048]{1,0:T(8,128)(2,1)S(1)}, u32[]{:S(2)}, u32[]{:S(2)}) collective-permute-start(bf16[16,2048]{1,0:T(8,128)(2,1)S(1)} %collective-permute-done.1), channel_id=1, source_target_pairs={{0,15},{1,0},{2,1},{3,2},{4,3},{5,4},{6,5},{7,6},{8,7},{9,8},{10,9... | collective-permute-start | bytes 196616 | tf_op jit(solution)/shard_map/ppermute | solution.py:25
  87.3 13.9 %collective-permute-start.19 = (bf16[16,2048]{1,0:T(8,128)(2,1)S(1)}, bf16[16,2048]{1,0:T(8,128)(2,1)S(1)}, u32[]{:S(2)}, u32[]{:S(2)}) collective-permute-start(bf16[16,2048]{1,0:T(8,128)(2,1)S(1)} %collective-permute-done.17), channel_id=1, source_target_pairs={{0,1},{1,2},{2,3},{3,4},{4,5},{5,6},{6,7},{7,8},{8,9},{9,10},{10,1... | collective-permute-start | bytes 196616 | tf_op jit(solution)/shard_map/ppermute | solution.py:20
  88.0 19.3 %collective-permute-start.20 = (bf16[16,2048]{1,0:T(8,128)(2,1)S(1)}, bf16[16,2048]{1,0:T(8,128)(2,1)S(1)}, u32[]{:S(2)}, u32[]{:S(2)}) collective-permute-start(bf16[16,2048]{1,0:T(8,128)(2,1)S(1)} %collective-permute-done.18), channel_id=1, source_target_pairs={{0,15},{1,0},{2,1},{3,2},{4,3},{5,4},{6,5},{7,6},{8,7},{9,8},{10,9... | collective-permute-start | bytes 196616 | tf_op jit(solution)/shard_map/ppermute | solution.py:25
  93.9 12.6 %collective-permute-start.34 = (bf16[16,2048]{1,0:T(8,128)(2,1)S(1)}, bf16[16,2048]{1,0:T(8,128)(2,1)S(1)}, u32[]{:S(2)}, u32[]{:S(2)}) collective-permute-start(bf16[16,2048]{1,0:T(8,128)(2,1)S(1)} %collective-permute-done.32), channel_id=1, source_target_pairs={{0,1},{1,2},{2,3},{3,4},{4,5},{5,6},{6,7},{7,8},{8,9},{9,10},{10,1... | collective-permute-start | bytes 196616 | tf_op jit(solution)/shard_map/ppermute | solution.py:20
  94.6 18.0 %collective-permute-start.35 = (bf16[16,2048]{1,0:T(8,128)(2,1)S(1)}, bf16[16,2048]{1,0:T(8,128)(2,1)S(1)}, u32[]{:S(2)}, u32[]{:S(2)}) collective-permute-start(bf16[16,2048]{1,0:T(8,128)(2,1)S(1)} %collective-permute-done.33), channel_id=1, source_target_pairs={{0,15},{1,0},{2,1},{3,2},{4,3},{5,4},{6,5},{7,6},{8,7},{9,8},{10,9... | collective-permute-start | bytes 196616 | tf_op jit(solution)/shard_map/ppermute | solution.py:25
  100.6 12.8 %collective-permute-start.49 = (bf16[16,2048]{1,0:T(8,128)(2,1)S(1)}, bf16[16,2048]{1,0:T(8,128)(2,1)S(1)}, u32[]{:S(2)}, u32[]{:S(2)}) collective-permute-start(bf16[16,2048]{1,0:T(8,128)(2,1)S(1)} %collective-permute-done.47), channel_id=1, source_target_pairs={{0,1},{1,2},{2,3},{3,4},{4,5},{5,6},{6,7},{7,8},{8,9},{9,10},{10,1... | collective-permute-start | bytes 196616 | tf_op jit(solution)/shard_map/ppermute | solution.py:20
  101.2 18.1 %collective-permute-start.50 = (bf16[16,2048]{1,0:T(8,128)(2,1)S(1)}, bf16[16,2048]{1,0:T(8,128)(2,1)S(1)}, u32[]{:S(2)}, u32[]{:S(2)}) collective-permute-start(bf16[16,2048]{1,0:T(8,128)(2,1)S(1)} %collective-permute-done.48), channel_id=1, source_target_pairs={{0,15},{1,0},{2,1},{3,2},{4,3},{5,4},{6,5},{7,6},{8,7},{9,8},{10,9... | collective-permute-start | bytes 196616 | tf_op jit(solution)/shard_map/ppermute | solution.py:25
  106.5 13.4 %collective-permute-start.4 = (bf16[16,2048]{1,0:T(8,128)(2,1)S(1)}, bf16[16,2048]{1,0:T(8,128)(2,1)S(1)}, u32[]{:S(2)}, u32[]{:S(2)}) collective-permute-start(bf16[16,2048]{1,0:T(8,128)(2,1)S(1)} %collective-permute-done.2), channel_id=1, source_target_pairs={{0,1},{1,2},{2,3},{3,4},{4,5},{5,6},{6,7},{7,8},{8,9},{9,10},{10,1... | collective-permute-start | bytes 196616 | tf_op jit(solution)/shard_map/ppermute | solution.py:20
  107.3 18.6 %collective-permute-start.5 = (bf16[16,2048]{1,0:T(8,128)(2,1)S(1)}, bf16[16,2048]{1,0:T(8,128)(2,1)S(1)}, u32[]{:S(2)}, u32[]{:S(2)}) collective-permute-start(bf16[16,2048]{1,0:T(8,128)(2,1)S(1)} %collective-permute-done.3), channel_id=1, source_target_pairs={{0,15},{1,0},{2,1},{3,2},{4,3},{5,4},{6,5},{7,6},{8,7},{9,8},{10,9... | collective-permute-start | bytes 196616 | tf_op jit(solution)/shard_map/ppermute | solution.py:25
  112.6 13.9 %collective-permute-start.21 = (bf16[16,2048]{1,0:T(8,128)(2,1)S(1)}, bf16[16,2048]{1,0:T(8,128)(2,1)S(1)}, u32[]{:S(2)}, u32[]{:S(2)}) collective-permute-start(bf16[16,2048]{1,0:T(8,128)(2,1)S(1)} %collective-permute-done.19), channel_id=1, source_target_pairs={{0,1},{1,2},{2,3},{3,4},{4,5},{5,6},{6,7},{7,8},{8,9},{9,10},{10,1... | collective-permute-start | bytes 196616 | tf_op jit(solution)/shard_map/ppermute | solution.py:20
  113.3 19.3 %collective-permute-start.22 = (bf16[16,2048]{1,0:T(8,128)(2,1)S(1)}, bf16[16,2048]{1,0:T(8,128)(2,1)S(1)}, u32[]{:S(2)}, u32[]{:S(2)}) collective-permute-start(bf16[16,2048]{1,0:T(8,128)(2,1)S(1)} %collective-permute-done.20), channel_id=1, source_target_pairs={{0,15},{1,0},{2,1},{3,2},{4,3},{5,4},{6,5},{7,6},{8,7},{9,8},{10,9... | collective-permute-start | bytes 196616 | tf_op jit(solution)/shard_map/ppermute | solution.py:25
  119.3 12.6 %collective-permute-start.36 = (bf16[16,2048]{1,0:T(8,128)(2,1)S(1)}, bf16[16,2048]{1,0:T(8,128)(2,1)S(1)}, u32[]{:S(2)}, u32[]{:S(2)}) collective-permute-start(bf16[16,2048]{1,0:T(8,128)(2,1)S(1)} %collective-permute-done.34), channel_id=1, source_target_pairs={{0,1},{1,2},{2,3},{3,4},{4,5},{5,6},{6,7},{7,8},{8,9},{9,10},{10,1... | collective-permute-start | bytes 196616 | tf_op jit(solution)/shard_map/ppermute | solution.py:20
  119.9 18.0 %collective-permute-start.37 = (bf16[16,2048]{1,0:T(8,128)(2,1)S(1)}, bf16[16,2048]{1,0:T(8,128)(2,1)S(1)}, u32[]{:S(2)}, u32[]{:S(2)}) collective-permute-start(bf16[16,2048]{1,0:T(8,128)(2,1)S(1)} %collective-permute-done.35), channel_id=1, source_target_pairs={{0,15},{1,0},{2,1},{3,2},{4,3},{5,4},{6,5},{7,6},{8,7},{9,8},{10,9... | collective-permute-start | bytes 196616 | tf_op jit(solution)/shard_map/ppermute | solution.py:25
  125.9 12.8 %collective-permute-start.51 = (bf16[16,2048]{1,0:T(8,128)(2,1)S(1)}, bf16[16,2048]{1,0:T(8,128)(2,1)S(1)}, u32[]{:S(2)}, u32[]{:S(2)}) collective-permute-start(bf16[16,2048]{1,0:T(8,128)(2,1)S(1)} %collective-permute-done.49), channel_id=1, source_target_pairs={{0,1},{1,2},{2,3},{3,4},{4,5},{5,6},{6,7},{7,8},{8,9},{9,10},{10,1... | collective-permute-start | bytes 196616 | tf_op jit(solution)/shard_map/ppermute | solution.py:20
  126.5 18.1 %collective-permute-start.52 = (bf16[16,2048]{1,0:T(8,128)(2,1)S(1)}, bf16[16,2048]{1,0:T(8,128)(2,1)S(1)}, u32[]{:S(2)}, u32[]{:S(2)}) collective-permute-start(bf16[16,2048]{1,0:T(8,128)(2,1)S(1)} %collective-permute-done.50), channel_id=1, source_target_pairs={{0,15},{1,0},{2,1},{3,2},{4,3},{5,4},{6,5},{7,6},{8,7},{9,8},{10,9... | collective-permute-start | bytes 196616 | tf_op jit(solution)/shard_map/ppermute | solution.py:25
  131.9 13.4 %collective-permute-start.6 = (bf16[16,2048]{1,0:T(8,128)(2,1)S(1)}, bf16[16,2048]{1,0:T(8,128)(2,1)S(1)}, u32[]{:S(2)}, u32[]{:S(2)}) collective-permute-start(bf16[16,2048]{1,0:T(8,128)(2,1)S(1)} %collective-permute-done.4), channel_id=1, source_target_pairs={{0,1},{1,2},{2,3},{3,4},{4,5},{5,6},{6,7},{7,8},{8,9},{9,10},{10,1... | collective-permute-start | bytes 196616 | tf_op jit(solution)/shard_map/ppermute | solution.py:20
  132.6 18.6 %collective-permute-start.7 = (bf16[16,2048]{1,0:T(8,128)(2,1)S(1)}, bf16[16,2048]{1,0:T(8,128)(2,1)S(1)}, u32[]{:S(2)}, u32[]{:S(2)}) collective-permute-start(bf16[16,2048]{1,0:T(8,128)(2,1)S(1)} %collective-permute-done.5), channel_id=1, source_target_pairs={{0,15},{1,0},{2,1},{3,2},{4,3},{5,4},{6,5},{7,6},{8,7},{9,8},{10,9... | collective-permute-start | bytes 196616 | tf_op jit(solution)/shard_map/ppermute | solution.py:25
  137.9 13.9 %collective-permute-start.23 = (bf16[16,2048]{1,0:T(8,128)(2,1)S(1)}, bf16[16,2048]{1,0:T(8,128)(2,1)S(1)}, u32[]{:S(2)}, u32[]{:S(2)}) collective-permute-start(bf16[16,2048]{1,0:T(8,128)(2,1)S(1)} %collective-permute-done.21), channel_id=1, source_target_pairs={{0,1},{1,2},{2,3},{3,4},{4,5},{5,6},{6,7},{7,8},{8,9},{9,10},{10,1... | collective-permute-start | bytes 196616 | tf_op jit(solution)/shard_map/ppermute | solution.py:20
  138.6 19.3 %collective-permute-start.24 = (bf16[16,2048]{1,0:T(8,128)(2,1)S(1)}, bf16[16,2048]{1,0:T(8,128)(2,1)S(1)}, u32[]{:S(2)}, u32[]{:S(2)}) collective-permute-start(bf16[16,2048]{1,0:T(8,128)(2,1)S(1)} %collective-permute-done.22), channel_id=1, source_target_pairs={{0,15},{1,0},{2,1},{3,2},{4,3},{5,4},{6,5},{7,6},{8,7},{9,8},{10,9... | collective-permute-start | bytes 196616 | tf_op jit(solution)/shard_map/ppermute | solution.py:25
  144.6 12.6 %collective-permute-start.38 = (bf16[16,2048]{1,0:T(8,128)(2,1)S(1)}, bf16[16,2048]{1,0:T(8,128)(2,1)S(1)}, u32[]{:S(2)}, u32[]{:S(2)}) collective-permute-start(bf16[16,2048]{1,0:T(8,128)(2,1)S(1)} %collective-permute-done.36), channel_id=1, source_target_pairs={{0,1},{1,2},{2,3},{3,4},{4,5},{5,6},{6,7},{7,8},{8,9},{9,10},{10,1... | collective-permute-start | bytes 196616 | tf_op jit(solution)/shard_map/ppermute | solution.py:20
  145.2 18.0 %collective-permute-start.39 = (bf16[16,2048]{1,0:T(8,128)(2,1)S(1)}, bf16[16,2048]{1,0:T(8,128)(2,1)S(1)}, u32[]{:S(2)}, u32[]{:S(2)}) collective-permute-start(bf16[16,2048]{1,0:T(8,128)(2,1)S(1)} %collective-permute-done.37), channel_id=1, source_target_pairs={{0,15},{1,0},{2,1},{3,2},{4,3},{5,4},{6,5},{7,6},{8,7},{9,8},{10,9... | collective-permute-start | bytes 196616 | tf_op jit(solution)/shard_map/ppermute | solution.py:25
  151.2 12.8 %collective-permute-start.53 = (bf16[16,2048]{1,0:T(8,128)(2,1)S(1)}, bf16[16,2048]{1,0:T(8,128)(2,1)S(1)}, u32[]{:S(2)}, u32[]{:S(2)}) collective-permute-start(bf16[16,2048]{1,0:T(8,128)(2,1)S(1)} %collective-permute-done.51), channel_id=1, source_target_pairs={{0,1},{1,2},{2,3},{3,4},{4,5},{5,6},{6,7},{7,8},{8,9},{9,10},{10,1... | collective-permute-start | bytes 196616 | tf_op jit(solution)/shard_map/ppermute | solution.py:20
  151.8 18.1 %collective-permute-start.54 = (bf16[16,2048]{1,0:T(8,128)(2,1)S(1)}, bf16[16,2048]{1,0:T(8,128)(2,1)S(1)}, u32[]{:S(2)}, u32[]{:S(2)}) collective-permute-start(bf16[16,2048]{1,0:T(8,128)(2,1)S(1)} %collective-permute-done.52), channel_id=1, source_target_pairs={{0,15},{1,0},{2,1},{3,2},{4,3},{5,4},{6,5},{7,6},{8,7},{9,8},{10,9... | collective-permute-start | bytes 196616 | tf_op jit(solution)/shard_map/ppermute | solution.py:25
  157.2 13.4 %collective-permute-start.8 = (bf16[16,2048]{1,0:T(8,128)(2,1)S(1)}, bf16[16,2048]{1,0:T(8,128)(2,1)S(1)}, u32[]{:S(2)}, u32[]{:S(2)}) collective-permute-start(bf16[16,2048]{1,0:T(8,128)(2,1)S(1)} %collective-permute-done.6), channel_id=1, source_target_pairs={{0,1},{1,2},{2,3},{3,4},{4,5},{5,6},{6,7},{7,8},{8,9},{9,10},{10,1... | collective-permute-start | bytes 196616 | tf_op jit(solution)/shard_map/ppermute | solution.py:20
  157.9 18.6 %collective-permute-start.9 = (bf16[16,2048]{1,0:T(8,128)(2,1)S(1)}, bf16[16,2048]{1,0:T(8,128)(2,1)S(1)}, u32[]{:S(2)}, u32[]{:S(2)}) collective-permute-start(bf16[16,2048]{1,0:T(8,128)(2,1)S(1)} %collective-permute-done.7), channel_id=1, source_target_pairs={{0,15},{1,0},{2,1},{3,2},{4,3},{5,4},{6,5},{7,6},{8,7},{9,8},{10,9... | collective-permute-start | bytes 196616 | tf_op jit(solution)/shard_map/ppermute | solution.py:25
  163.2 13.9 %collective-permute-start.25 = (bf16[16,2048]{1,0:T(8,128)(2,1)S(1)}, bf16[16,2048]{1,0:T(8,128)(2,1)S(1)}, u32[]{:S(2)}, u32[]{:S(2)}) collective-permute-start(bf16[16,2048]{1,0:T(8,128)(2,1)S(1)} %collective-permute-done.23), channel_id=1, source_target_pairs={{0,1},{1,2},{2,3},{3,4},{4,5},{5,6},{6,7},{7,8},{8,9},{9,10},{10,1... | collective-permute-start | bytes 196616 | tf_op jit(solution)/shard_map/ppermute | solution.py:20
  164.0 19.5 %collective-permute-start.26 = (bf16[16,2048]{1,0:T(8,128)(2,1)S(1)}, bf16[16,2048]{1,0:T(8,128)(2,1)S(1)}, u32[]{:S(2)}, u32[]{:S(2)}) collective-permute-start(bf16[16,2048]{1,0:T(8,128)(2,1)S(1)} %collective-permute-done.24), channel_id=1, source_target_pairs={{0,15},{1,0},{2,1},{3,2},{4,3},{5,4},{6,5},{7,6},{8,7},{9,8},{10,9... | collective-permute-start | bytes 196616 | tf_op jit(solution)/shard_map/ppermute | solution.py:25
  169.9 12.8 %collective-permute-start.40 = (bf16[16,2048]{1,0:T(8,128)(2,1)S(1)}, bf16[16,2048]{1,0:T(8,128)(2,1)S(1)}, u32[]{:S(2)}, u32[]{:S(2)}) collective-permute-start(bf16[16,2048]{1,0:T(8,128)(2,1)S(1)} %collective-permute-done.38), channel_id=1, source_target_pairs={{0,1},{1,2},{2,3},{3,4},{4,5},{5,6},{6,7},{7,8},{8,9},{9,10},{10,1... | collective-permute-start | bytes 196616 | tf_op jit(solution)/shard_map/ppermute | solution.py:20
  170.5 18.2 %collective-permute-start.41 = (bf16[16,2048]{1,0:T(8,128)(2,1)S(1)}, bf16[16,2048]{1,0:T(8,128)(2,1)S(1)}, u32[]{:S(2)}, u32[]{:S(2)}) collective-permute-start(bf16[16,2048]{1,0:T(8,128)(2,1)S(1)} %collective-permute-done.39), channel_id=1, source_target_pairs={{0,15},{1,0},{2,1},{3,2},{4,3},{5,4},{6,5},{7,6},{8,7},{9,8},{10,9... | collective-permute-start | bytes 196616 | tf_op jit(solution)/shard_map/ppermute | solution.py:25
  176.5 13.0 %collective-permute-start.55 = (bf16[16,2048]{1,0:T(8,128)(2,1)S(1)}, bf16[16,2048]{1,0:T(8,128)(2,1)S(1)}, u32[]{:S(2)}, u32[]{:S(2)}) collective-permute-start(bf16[16,2048]{1,0:T(8,128)(2,1)S(1)} %collective-permute-done.53), channel_id=1, source_target_pairs={{0,1},{1,2},{2,3},{3,4},{4,5},{5,6},{6,7},{7,8},{8,9},{9,10},{10,1... | collective-permute-start | bytes 196616 | tf_op jit(solution)/shard_map/ppermute | solution.py:20
  177.1 18.3 %collective-permute-start.56 = (bf16[16,2048]{1,0:T(8,128)(2,1)S(1)}, bf16[16,2048]{1,0:T(8,128)(2,1)S(1)}, u32[]{:S(2)}, u32[]{:S(2)}) collective-permute-start(bf16[16,2048]{1,0:T(8,128)(2,1)S(1)} %collective-permute-done.54), channel_id=1, source_target_pairs={{0,15},{1,0},{2,1},{3,2},{4,3},{5,4},{6,5},{7,6},{8,7},{9,8},{10,9... | collective-permute-start | bytes 196616 | tf_op jit(solution)/shard_map/ppermute | solution.py:25
  182.7 13.4 %collective-permute-start.10 = (bf16[16,2048]{1,0:T(8,128)(2,1)S(1)}, bf16[16,2048]{1,0:T(8,128)(2,1)S(1)}, u32[]{:S(2)}, u32[]{:S(2)}) collective-permute-start(bf16[16,2048]{1,0:T(8,128)(2,1)S(1)} %collective-permute-done.8), channel_id=1, source_target_pairs={{0,1},{1,2},{2,3},{3,4},{4,5},{5,6},{6,7},{7,8},{8,9},{9,10},{10,1... | collective-permute-start | bytes 196616 | tf_op jit(solution)/shard_map/ppermute | solution.py:20
  183.4 18.6 %collective-permute-start.11 = (bf16[16,2048]{1,0:T(8,128)(2,1)S(1)}, bf16[16,2048]{1,0:T(8,128)(2,1)S(1)}, u32[]{:S(2)}, u32[]{:S(2)}) collective-permute-start(bf16[16,2048]{1,0:T(8,128)(2,1)S(1)} %collective-permute-done.9), channel_id=1, source_target_pairs={{0,15},{1,0},{2,1},{3,2},{4,3},{5,4},{6,5},{7,6},{8,7},{9,8},{10,9... | collective-permute-start | bytes 196616 | tf_op jit(solution)/shard_map/ppermute | solution.py:25
  188.8 13.9 %collective-permute-start.27 = (bf16[16,2048]{1,0:T(8,128)(2,1)S(1)}, bf16[16,2048]{1,0:T(8,128)(2,1)S(1)}, u32[]{:S(2)}, u32[]{:S(2)}) collective-permute-start(bf16[16,2048]{1,0:T(8,128)(2,1)S(1)} %collective-permute-done.25), channel_id=1, source_target_pairs={{0,1},{1,2},{2,3},{3,4},{4,5},{5,6},{6,7},{7,8},{8,9},{9,10},{10,1... | collective-permute-start | bytes 196616 | tf_op jit(solution)/shard_map/ppermute | solution.py:20
  189.5 19.3 %collective-permute-start.28 = (bf16[16,2048]{1,0:T(8,128)(2,1)S(1)}, bf16[16,2048]{1,0:T(8,128)(2,1)S(1)}, u32[]{:S(2)}, u32[]{:S(2)}) collective-permute-start(bf16[16,2048]{1,0:T(8,128)(2,1)S(1)} %collective-permute-done.26), channel_id=1, source_target_pairs={{0,15},{1,0},{2,1},{3,2},{4,3},{5,4},{6,5},{7,6},{8,7},{9,8},{10,9... | collective-permute-start | bytes 196616 | tf_op jit(solution)/shard_map/ppermute | solution.py:25
  195.4 12.6 %collective-permute-start.42 = (bf16[16,2048]{1,0:T(8,128)(2,1)S(1)}, bf16[16,2048]{1,0:T(8,128)(2,1)S(1)}, u32[]{:S(2)}, u32[]{:S(2)}) collective-permute-start(bf16[16,2048]{1,0:T(8,128)(2,1)S(1)} %collective-permute-done.40), channel_id=1, source_target_pairs={{0,1},{1,2},{2,3},{3,4},{4,5},{5,6},{6,7},{7,8},{8,9},{9,10},{10,1... | collective-permute-start | bytes 196616 | tf_op jit(solution)/shard_map/ppermute | solution.py:20
  196.1 18.0 %collective-permute-start.43 = (bf16[16,2048]{1,0:T(8,128)(2,1)S(1)}, bf16[16,2048]{1,0:T(8,128)(2,1)S(1)}, u32[]{:S(2)}, u32[]{:S(2)}) collective-permute-start(bf16[16,2048]{1,0:T(8,128)(2,1)S(1)} %collective-permute-done.41), channel_id=1, source_target_pairs={{0,15},{1,0},{2,1},{3,2},{4,3},{5,4},{6,5},{7,6},{8,7},{9,8},{10,9... | collective-permute-start | bytes 196616 | tf_op jit(solution)/shard_map/ppermute | solution.py:25
  202.0 12.8 %collective-permute-start.57 = (bf16[16,2048]{1,0:T(8,128)(2,1)S(1)}, bf16[16,2048]{1,0:T(8,128)(2,1)S(1)}, u32[]{:S(2)}, u32[]{:S(2)}) collective-permute-start(bf16[16,2048]{1,0:T(8,128)(2,1)S(1)} %collective-permute-done.55), channel_id=1, source_target_pairs={{0,1},{1,2},{2,3},{3,4},{4,5},{5,6},{6,7},{7,8},{8,9},{9,10},{10,1... | collective-permute-start | bytes 196616 | tf_op jit(solution)/shard_map/ppermute | solution.py:20
  202.7 13.7 %collective-permute-start.58 = (bf16[16,2048]{1,0:T(8,128)(2,1)S(1)}, bf16[16,2048]{1,0:T(8,128)(2,1)S(1)}, u32[]{:S(2)}, u32[]{:S(2)}) collective-permute-start(bf16[16,2048]{1,0:T(8,128)(2,1)S(1)} %collective-permute-done.56), channel_id=1, source_target_pairs={{0,15},{1,0},{2,1},{3,2},{4,3},{5,4},{6,5},{7,6},{8,7},{9,8},{10,9... | collective-permute-start | bytes 196616 | tf_op jit(solution)/shard_map/ppermute | solution.py:25
  330.9 16.7 %all-to-all-start = ((bf16[60,16,512]{2,0,1:T(8,128)(2,1)}), bf16[60,16,512]{2,0,1:T(8,128)(2,1)S(1)}, u32[]{:S(2)}, u32[]{:S(2)}) async-start(bf16[60,16,512]{2,0,1:T(8,128)(2,1)} %fusion.20), calls=%async_computation | async-start | bytes 2097152 | tf_op jit(solution)/shard_map/all_to_all | solution.py:145
  334.7 101.2 %all-reduce.11.cloned.1.call-start = ((), (), s32[]{:S(2)}) async-start(), calls=%async_computation.8 | async-start | bytes 655360 | tf_op jit(solution)/shard_map/psum | solution.py:120
  338.4 111.9 %all-gather.21.cloned.1.call-start = ((), (), s32[]{:S(2)}) async-start(), calls=%async_computation.4 | async-start | bytes 3145728 | tf_op jit(solution)/shard_map/all_gather | solution.py:146
  352.3 16.6 %all-to-all-start.1 = ((bf16[60,16,512]{2,0,1:T(8,128)(2,1)}), bf16[60,16,512]{2,0,1:T(8,128)(2,1)S(1)}, u32[]{:S(2)}, u32[]{:S(2)}) async-start(bf16[60,16,512]{2,0,1:T(8,128)(2,1)} %fusion.21), calls=%async_computation.1 | async-start | bytes 2097152 | tf_op jit(solution)/shard_map/all_to_all | solution.py:145
  356.0 169.5 %all-gather.23.cloned.1.call-start = ((), (), s32[]{:S(2)}) async-start(), calls=%async_computation.5 | async-start | bytes 3145728 | tf_op jit(solution)/shard_map/all_gather | solution.py:146
  373.7 16.8 %all-to-all-start.2 = ((bf16[60,16,512]{2,0,1:T(8,128)(2,1)}), bf16[60,16,512]{2,0,1:T(8,128)(2,1)S(1)}, u32[]{:S(2)}, u32[]{:S(2)}) async-start(bf16[60,16,512]{2,0,1:T(8,128)(2,1)} %fusion.22), calls=%async_computation.2 | async-start | bytes 2097152 | tf_op jit(solution)/shard_map/all_to_all | solution.py:145
  377.4 222.7 %all-gather.25.cloned.1.call-start = ((), (), s32[]{:S(2)}) async-start(), calls=%async_computation.6 | async-start | bytes 3145728 | tf_op jit(solution)/shard_map/all_gather | solution.py:146
  395.2 51.9 %all-to-all-start.3 = ((bf16[60,16,512]{2,0,1:T(8,128)(2,1)}), bf16[60,16,512]{2,0,1:T(8,128)(2,1)S(1)}, u32[]{:S(2)}, u32[]{:S(2)}) async-start(bf16[60,16,512]{2,0,1:T(8,128)(2,1)} %fusion.23), calls=%async_computation.3 | async-start | bytes 2097152 | tf_op jit(solution)/shard_map/all_to_all | solution.py:145
  398.8 276.1 %all-gather.27.cloned.1.call-start = ((), (), s32[]{:S(2)}) async-start(), calls=%async_computation.7 | async-start | bytes 3145728 | tf_op jit(solution)/shard_map/all_gather | solution.py:146
  (33 other events, 785.6 us)
Sparse Core Ops, SparseCore 0:
  229.9 56.0 all-reduce.12
  339.1 96.8 all-reduce.10
  437.6 12.7 all-gather.20
  451.8 14.6 all-gather.22
  468.0 14.6 all-gather.24
  484.1 14.6 all-gather.26
